TPU v7x, 32 devices: a whole 2x2x4 slice. The times are simulated.
32 devices in a mesh: ctx: 8 (over z, y), grp: 4 (over x, core).
Axes of the slice: x: 2, y: 2, z: 4, core: 2. Of those that a mesh axis runs over, the one named last changes fastest.
Arguments:
- channels: bfloat16 [4096, 5120], P(('ctx', 'grp')), may hold values from -6 to 6
- gates: bfloat16 [4096, 5120], P(('ctx', 'grp')), may hold values from -6 to 6
- b_proj: bfloat16 [4096, 128], P(('ctx', 'grp')), may hold values from -6 to 6
- c_proj: bfloat16 [4096, 128], P(('ctx', 'grp')), may hold values from -0.5 to 0.5
- step_size: bfloat16 [4096, 80], P(('ctx', 'grp')), may hold values from 0.001 to 1, as said below
- log_decay: bfloat16 [4096, 80], P(('ctx', 'grp')), may hold values from -1 to 0, as said below
- skip_gain: float32 [80], P('grp'), may hold values from 0.5 to 2
- norm_gain: float32 [5120], P('grp'), may hold values from 0.1 to 1.9
- out_weight: bfloat16 [5120, 2560], P('grp'), may hold values from -0.078125 to 0.078125
Outputs:
- layer_out: bfloat16 [4096, 2560], P(('ctx', 'grp'))
Inputs may be any that keep to these rules, and one draw needn't show every extreme that they name: `step_size`: each token's step of each head is positive. `log_decay`: each token's log decay of each head is negative.
All inputs are finite; a program needn't handle non-finite values.
Results may differ from a plain program's by a relative error of at most 0.009.
Values may be sent and summed in bfloat16 or wider, within the bound.
A program may use at most 128 MiB of HBM per device.

v0:
```python
import jax
import jax.numpy as jnp
from jax import lax
from jax.sharding import PartitionSpec as P

HEADS = 80
HD = 64
NSTATE = 128
GROUP = 256


def prefix_2(value, axis, join, neutral):
    count, mine = (lax.axis_size(axis), lax.axis_index(axis))
    pieces = jax.tree.map(lambda part: lax.all_gather(part, axis), value)
    so_far = jax.tree.map(
        lambda part, zero: jnp.full_like(part, 0) + jnp.asarray(zero, part.dtype), value, neutral
    )

    def turn(position, so_far):
        longer = join(so_far, jax.tree.map(lambda part: part[position], pieces))
        return jax.tree.map(lambda new, old: jnp.where(position < mine, new, old), longer, so_far)

    return lax.fori_loop(0, count - 1, turn, so_far)


def local_scan(chan_heads, step_heads, decay_heads, b_rows, c_rows):
    highest = lax.Precision.HIGHEST
    piece_len = chan_heads.shape[0]
    nheads = step_heads.shape[1]
    blocks = piece_len // GROUP
    running = jnp.cumsum(decay_heads.astype(jnp.float32).reshape(blocks, GROUP, nheads), axis=1)
    running_t = jnp.transpose(running, (0, 2, 1))
    chan_f = chan_heads.astype(jnp.float32).reshape(piece_len, nheads, HD)
    inputs = (chan_f * step_heads.astype(jnp.float32)[:, :, None]).reshape(
        blocks, GROUP, nheads, HD
    )
    b_blocks = b_rows.reshape(blocks, GROUP, NSTATE)
    c_blocks = c_rows.reshape(blocks, GROUP, NSTATE)
    scores = jnp.einsum("qin,qjn->qij", c_blocks, b_blocks, preferred_element_type=jnp.float32)
    rows_at = lax.broadcasted_iota(jnp.int32, (GROUP, GROUP), 0)
    cols_at = lax.broadcasted_iota(jnp.int32, (GROUP, GROUP), 1)
    causal = rows_at >= cols_at
    spread = running_t[:, :, :, None] - running_t[:, :, None, :]
    weights = jnp.where(causal[None, None], jnp.exp(spread), 0.0) * scores[:, None]
    y_intra = jnp.einsum("qhij,qjhp->qihp", weights, inputs, precision=highest)
    tail_decay = jnp.exp(running[:, -1:, :] - running)
    b_float = b_blocks.astype(jnp.float32)
    c_float = c_blocks.astype(jnp.float32)
    group_states = jnp.einsum(
        "qjhp,qjn->qhpn", inputs * tail_decay[..., None], b_float, precision=highest
    )
    totals = jnp.exp(running[:, -1, :])

    def carry_step(carried, packed):
        factor, fresh_state = packed
        return (factor[:, None, None] * carried + fresh_state, carried)

    final_state, starts = lax.scan(
        carry_step, jnp.zeros((nheads, HD, NSTATE), jnp.float32), (totals, group_states)
    )
    y_inter = (
        jnp.einsum("qin,qhpn->qihp", c_float, starts, precision=highest)
        * jnp.exp(running)[..., None]
    )
    group_logs = running[:, -1, :]
    offsets = jnp.cumsum(group_logs, axis=0) - group_logs
    piece_cum = (running + offsets[:, None, :]).reshape(piece_len, nheads)
    piece_log = jnp.sum(group_logs, axis=0)
    local_out = (y_intra + y_inter).reshape(piece_len, nheads, HD)
    return (local_out, final_state, piece_log, piece_cum, chan_f)


def local(channels, gates, b_proj, c_proj, step_size, log_decay, skip_gain, norm_gain, out_weight):
    highest = lax.Precision.HIGHEST
    chan_heads, gate_heads, step_heads, decay_heads = (
        lax.all_to_all(channels, "grp", split_axis=1, concat_axis=0, tiled=True),
        lax.all_to_all(gates, "grp", split_axis=1, concat_axis=0, tiled=True),
        lax.all_to_all(step_size, "grp", split_axis=1, concat_axis=0, tiled=True),
        lax.all_to_all(log_decay, "grp", split_axis=1, concat_axis=0, tiled=True),
    )
    b_rows, c_rows = (
        lax.all_gather(b_proj, "grp", axis=0, tiled=True),
        lax.all_gather(c_proj, "grp", axis=0, tiled=True),
    )
    local_out, final_state, piece_log, piece_cum, chan_f = local_scan(
        chan_heads, step_heads, decay_heads, b_rows, c_rows
    )
    piece_factor = jnp.exp(piece_log)

    def combine(early_part, later_part):
        return (
            early_part[0] * later_part[0],
            later_part[0][:, None, None] * early_part[1] + later_part[1],
        )

    identity = (jnp.ones_like(piece_factor), jnp.zeros_like(final_state))
    prefix = prefix_2((piece_factor, final_state), "ctx", combine, identity)
    incoming = prefix[1]
    correction = jnp.einsum("tn,hpn->thp", c_rows.astype(jnp.float32), incoming, precision=highest)
    correction = correction * jnp.exp(piece_cum)[:, :, None]
    ssm_out = local_out + correction + skip_gain[None, :, None] * chan_f
    piece_len = chan_heads.shape[0]
    gated_out = ssm_out.reshape(piece_len, chan_heads.shape[1]) * jax.nn.silu(
        gate_heads.astype(jnp.float32)
    )
    row_squares = lax.psum(jnp.sum(gated_out * gated_out, axis=1), "grp")
    scale = lax.rsqrt(row_squares / (HEADS * HD) + 1e-05)
    normed = (gated_out * scale[:, None] * norm_gain[None, :]).astype(jnp.bfloat16)
    return lax.psum_scatter(
        jnp.dot(normed, out_weight, preferred_element_type=jnp.float32).astype(jnp.bfloat16),
        "grp",
        scatter_dimension=0,
        tiled=True,
    )


def solution(mesh):
    in_specs = (
        P(("ctx", "grp"), None),
        P(("ctx", "grp"), None),
        P(("ctx", "grp"), None),
        P(("ctx", "grp"), None),
        P(("ctx", "grp"), None),
        P(("ctx", "grp"), None),
        P("grp"),
        P("grp"),
        P("grp", None),
    )
    out_specs = P(("ctx", "grp"), None)
    return jax.shard_map(local, mesh=mesh, in_specs=in_specs, out_specs=out_specs, check_vma=False)
```

profile of v0, /device:TPU:0, one launch (start us, length us, event | category | flops | bytes accessed | tf_op | source)
XLA Modules:
  0.0 233.1 jit_solution(6459703165636211416)
XLA Ops:
  7.9 4.2 %all-to-all-start.2 = ((bf16[128,4,20]{0,2,1:T(8,128)(2,1)}), bf16[128,4,20]{0,2,1:T(8,128)(2,1)S(1)}, u32[]{:S(2)}, u32[]{:S(2)}) async-start(bf16[128,4,20]{0,2,1:T(8,128)(2,1)} %all_to_all.44), calls=%async_computation.2 | async-start | bytes 49152 | tf_op jit(solution)/shard_map/all_to_all | solution.py:79
  12.1 5.8 %all_gather.17 = bf16[512,128]{1,0:T(8,128)(2,1)S(1)} all-gather(bf16[128,128]{1,0:T(8,128)(2,1)} %param.15), channel_id=1, replica_groups=mesh['ctx'=8,'grp'=4] {'grp'}, dimensions={0}, use_global_device_ids=true | all-gather | bytes 163840 | tf_op jit(solution)/shard_map/all_gather | solution.py:82
  20.9 3.3 %all-to-all-start.1 = ((bf16[128,4,20]{0,2,1:T(8,128)(2,1)}), bf16[128,4,20]{0,2,1:T(8,128)(2,1)S(1)}, u32[]{:S(2)}, u32[]{:S(2)}) async-start(bf16[128,4,20]{0,2,1:T(8,128)(2,1)} %all_to_all.42), calls=%async_computation.1 | async-start | bytes 49152 | tf_op jit(solution)/shard_map/all_to_all | solution.py:78
  28.1 3.5 %all-to-all-start = ((bf16[128,4,1280]{0,2,1:T(8,128)(2,1)}), bf16[128,4,1280]{0,2,1:T(8,128)(2,1)S(1)}, u32[]{:S(2)}, u32[]{:S(2)}) async-start(bf16[128,4,1280]{0,2,1:T(8,128)(2,1)} %bitcast), calls=%async_computation | async-start | bytes 2621440 | tf_op jit(solution)/shard_map/all_to_all | solution.py:76
  33.5 15.3 %all-to-all-done = bf16[128,4,1280]{0,2,1:T(8,128)(2,1)S(1)} async-done(((bf16[128,4,1280]{0,2,1:T(8,128)(2,1)}), bf16[128,4,1280]{0,2,1:T(8,128)(2,1)S(1)}, u32[]{:S(2)}, u32[]{:S(2)}) %all-to-all-start) | async-done | bytes 1310752 | tf_op jit(solution)/shard_map/all_to_all | solution.py:76
  49.0 5.4 %copy.52 = f32[4,128,1280]{1,0,2:T(4,128)S(1)} copy(f32[4,128,1280]{1,2,0:T(8,128)S(1)} %convert_bitcast_fusion.1) | data formatting | bytes 5242880 | tf_op jit(solution)/shard_map/convert_element_type | solution.py:33
  54.5 3.3 %reshape.122 = f32[2,256,20,64]{1,0,3,2:T(2,128)} reshape(f32[4,128,1280]{1,0,2:T(4,128)S(1)} %copy.52) | data formatting | bytes 5242880 | tf_op jit(solution)/shard_map/convert_element_type | solution.py:33
  57.8 5.1 %broadcast_multiply_fusion = (f32[2,256,20,64]{1,0,3,2:T(2,128)S(1)}, f32[2,256,20,64]{1,0,3,2:T(2,128)}) fusion(f32[2,256,20]{1,0,2:T(2,128)S(1)} %get-tuple-element.189, f32[2,256,20,64]{1,0,3,2:T(2,128)} %reshape.122, f32[2,256,20]{1,0,2:T(2,128)S(1)} %reshape.123), kind=kLoop, calls=%fused_computation.39 | loop fusion | flops 1310720 | bytes 7946240 | tf_op jit(solution)/shard_map/mul | solution.py:50
  65.3 4.3 %while.27 = (s32[]{:T(128)}, f32[20,64,128]{2,1,0:T(8,128)S(1)}, f32[2,20,64,128]{3,2,1,0:T(8,128)}, f32[2,20]{1,0:T(2,128)S(1)}, f32[2,20,64,128]{3,2,1,0:T(8,128)}, /*index=5*/s32[]{:T(128)}, s32[]{:T(128)}) while((s32[]{:T(128)}, f32[20,64,128]{2,1,0:T(8,128)S(1)}, f32[2,20,64,128]{3,2,1,0:T(8,128)}, f32[2,20]{1,0:T(2,128)S(1)}, ...), condition=%wide.region_3.4_spmd.clone, body=%wide.region_2.3_spmd.clone.sunk | while | flops 655363 | bytes 3277648 | solution.py:58
  70.5 2.5 %copy.68 = bf16[128,5120]{0,1:T(8,128)(2,1)} copy(bf16[128,5120]{1,0:T(8,128)(2,1)} %param.14) | data formatting | bytes 2621440 | tf_op args[1]
  72.9 4.3 %all-to-all-start.3 = ((bf16[128,4,1280]{0,2,1:T(8,128)(2,1)}), bf16[128,4,1280]{0,2,1:T(8,128)(2,1)}, u32[]{:S(2)}, u32[]{:S(2)}) async-start(bf16[128,4,1280]{0,2,1:T(8,128)(2,1)} %bitcast.127), calls=%async_computation.3 | async-start | bytes 2621440 | tf_op jit(solution)/shard_map/all_to_all | solution.py:77
  78.5 17.5 %all_gather.16 = bf16[512,128]{1,0:T(8,128)(2,1)S(1)} all-gather(bf16[128,128]{1,0:T(8,128)(2,1)} %param.16), channel_id=1, replica_groups=mesh['ctx'=8,'grp'=4] {'grp'}, dimensions={0}, use_global_device_ids=true | all-gather | bytes 163840 | tf_op jit(solution)/shard_map/all_gather | solution.py:83
  100.0 22.7 %all-reduce = f32[160]{0:T(256)S(1)} all-reduce(f32[160]{0:T(256)S(1)} %exponential_dynamic-update-slice_fusion), channel_id=2, replica_groups=mesh['ctx'=8,'grp'=4] {'ctx'}, use_global_device_ids=true, to_apply=%add | all-reduce | flops 160 | bytes 1280
  126.3 13.1 %fusion.2 = f32[2,20,64,256]{3,2,1,0:T(8,128)S(1)} fusion(f32[2,256,256]{2,1,0:T(8,128)} %fusion.28, f32[2,20,256]{2,1,0:T(8,128)} %copy.57, pred[256,256]{1,0:T(8,128)(4,1)S(1)} %copy-done.3, f32[2,256,20,64]{1,0,3,2:T(2,128)} %get-tuple-element.187), kind=kOutput, calls=%fused_computation.7 | convolution fusion | flops 2021130240 | bytes 5873664 | tf_op jit(solution)/shard_map/qhij,qjhp->qihp/dot_general | solution.py:45
  146.1 4.1 %copy.71 = f32[4,128,1280]{1,0,2:T(4,128)} copy(f32[4,128,1280]{2,1,0:T(8,128)} %convert_bitcast_fusion) | data formatting | bytes 5242880 | tf_op jit(solution)/shard_map/convert_element_type | solution.py:104
  150.2 4.1 %reshape.127 = f32[512,20,64]{0,2,1:T(8,128)} reshape(f32[4,128,1280]{1,0,2:T(4,128)} %copy.71) | data formatting | bytes 5242880 | tf_op jit(solution)/shard_map/convert_element_type | solution.py:104
  154.4 3.5 %all-gather.4.cloned.1.call-done = f32[160,64,128]{2,1,0:T(8,128)} async-done(((f32[20,64,128]{2,1,0:T(8,128)}), f32[160,64,128]{2,1,0:T(8,128)}) %all-gather.4.cloned.1.call-update) | async-done | bytes 5242896 | tf_op jit(solution)/shard_map/all_gather | solution.py:14
  157.9 8.9 %while.28 = (s32[]{:T(128)}, f32[20,64,128]{2,1,0:T(8,128)S(1)}, s32[]{:T(128)}, f32[8,20]{1,0:T(8,128)S(1)}, f32[8,20,64,128]{3,2,1,0:T(8,128)}, /*index=5*/s32[]{:T(128)}, s32[]{:T(128)}) while((s32[]{:T(128)}, f32[20,64,128]{2,1,0:T(8,128)S(1)}, s32[]{:T(128)}, f32[8,20]{1,0:T(8,128)S(1)}, f32[8,20,64,128]{3,2,1,0:T(8,128)}, ...), condition=%wide.region_6.7_spmd.clone, body=%wide.region_5.6_spmd.clone.sunk | while | flops 655364 | bytes 1966425 | solution.py:23
  166.8 6.9 %multiply_reduce_fusion = (f32[512]{0:T(512)S(1)}, f32[512,20,64]{0,2,1:T(8,128)}) fusion(f32[512,20,64]{0,2,1:T(8,128)} %reshape.127, f32[512,20,64]{0,2,1:T(8,128)} %reshape.125, f32[20]{0:T(128)S(1)} %copy-done.7, f32[512,20,64]{0,2,1:T(8,128)} %bitcast.128, f32[512,20]{0,1:T(8,128)S(1)} %bitcast.139, f32[20,64,128]{2,1,0:T(8,128)S(1)} %get-tuple-element.129, ...), kind=kOutput, calls=%fused_computation.37 | convolution fusion | flops 1013841408 | bytes 11315280 | tf_op jit(solution)/shard_map/tn,hpn->thp/dot_general | solution.py:99
  173.7 3.2 %copy.70 = f32[512,1280]{1,0:T(8,128)} copy(f32[512,1280]{0,1:T(8,128)} %bitcast.129) | data formatting | bytes 5242880 | tf_op jit(solution)/shard_map/reshape | solution.py:103
  176.9 5.9 %psum.7 = f32[512]{0:T(512)S(1)} all-reduce(f32[512]{0:T(512)S(1)} %get-tuple-element.193), channel_id=1, replica_groups=mesh['ctx'=8,'grp'=4] {'grp'}, use_global_device_ids=true, to_apply=%region_9.10 | all-reduce | flops 512 | bytes 4096 | tf_op jit(solution)/shard_map/psum | solution.py:106
  182.9 2.6 %fusion.25 = bf16[512,1280]{1,0:T(8,128)(2,1)S(1)} fusion(f32[512,1280]{1,0:T(8,128)} %copy.70, bf16[128,4,1280]{2,0,1:T(8,128)(2,1)S(1)} %copy.69, f32[1280]{0:T(1024)S(1)} %copy-done.6, f32[512]{0:T(512)S(1)} %add_rsqrt_fusion), kind=kLoop, calls=%fused_computation.38 | loop fusion | flops 5898240 | bytes 5250048 | tf_op jit(solution)/shard_map/convert_element_type | solution.py:108
  185.5 7.7 %convolution_convert_fusion = bf16[512,2560]{1,0:T(8,128)(2,1)} fusion(bf16[512,1280]{1,0:T(8,128)(2,1)S(1)} %fusion.25, bf16[1280,2560]{1,0:T(8,128)(2,1)} %param.21), kind=kOutput, calls=%fused_computation.17 | convolution fusion | flops 3356753920 | bytes 10485760 | tf_op jit(solution)/shard_map/dot_general | solution.py:110
  193.2 33.1 %reduce-scatter.2.cloned.1.call-done = bf16[128,2560]{1,0:T(8,128)(2,1)} async-done(((bf16[512,2560]{1,0:T(8,128)(2,1)}), bf16[128,2560]{1,0:T(8,128)(2,1)}) %reduce-scatter.2.cloned.1.call-update) | async-done | bytes 655376 | tf_op jit(solution)/shard_map/reduce_scatter | solution.py:109
  (93 shorter events, 41.3 us)
Async XLA Ops:
  6.5 13.8 %copy-start.5 = (bf16[128,80]{0,1:T(8,128)(2,1)S(1)}, bf16[128,80]{0,1:T(8,128)(2,1)}, u32[]{:S(2)}) copy-start(bf16[128,80]{0,1:T(8,128)(2,1)} %param.17) | copy-start | bytes 61444
  7.9 13.0 %all-to-all-start.2 = ((bf16[128,4,20]{0,2,1:T(8,128)(2,1)}), bf16[128,4,20]{0,2,1:T(8,128)(2,1)S(1)}, u32[]{:S(2)}, u32[]{:S(2)}) async-start(bf16[128,4,20]{0,2,1:T(8,128)(2,1)} %all_to_all.44), calls=%async_computation.2 | async-start | bytes 49152 | tf_op jit(solution)/shard_map/all_to_all | solution.py:79
  20.9 7.1 %all-to-all-start.1 = ((bf16[128,4,20]{0,2,1:T(8,128)(2,1)}), bf16[128,4,20]{0,2,1:T(8,128)(2,1)S(1)}, u32[]{:S(2)}, u32[]{:S(2)}) async-start(bf16[128,4,20]{0,2,1:T(8,128)(2,1)} %all_to_all.42), calls=%async_computation.1 | async-start | bytes 49152 | tf_op jit(solution)/shard_map/all_to_all | solution.py:78
  28.1 20.8 %all-to-all-start = ((bf16[128,4,1280]{0,2,1:T(8,128)(2,1)}), bf16[128,4,1280]{0,2,1:T(8,128)(2,1)S(1)}, u32[]{:S(2)}, u32[]{:S(2)}) async-start(bf16[128,4,1280]{0,2,1:T(8,128)(2,1)} %bitcast), calls=%async_computation | async-start | bytes 2621440 | tf_op jit(solution)/shard_map/all_to_all | solution.py:76
  31.6 126.3 %all-gather.4.cloned.1.call-start = ((), (), s32[]{:S(2)}) async-start(), calls=%async_computation.6 | async-start | bytes 5898240 | tf_op jit(solution)/shard_map/all_gather | solution.py:14
  31.8 17.0 %copy-start.2 = (f32[2,20,256]{2,0,1:T(2,128)}, f32[2,20,256]{2,0,1:T(2,128)S(1)}, u32[]{:S(2)}) copy-start(f32[2,20,256]{2,0,1:T(2,128)S(1)} %reduce_window_sum.35) | copy-start | bytes 122884
  69.6 0.8 copy-start
  70.5 6.9 %copy-start.8 = (u32[32]{0:T(128)S(1)}, u32[32]{0:T(128)}, u32[]{:S(2)}) copy-start(u32[32]{0:T(128)} %constant.61) | copy-start | bytes 388
  72.9 69.8 %all-to-all-start.3 = ((bf16[128,4,1280]{0,2,1:T(8,128)(2,1)}), bf16[128,4,1280]{0,2,1:T(8,128)(2,1)}, u32[]{:S(2)}, u32[]{:S(2)}) async-start(bf16[128,4,1280]{0,2,1:T(8,128)(2,1)} %bitcast.127), calls=%async_computation.3 | async-start | bytes 2621440 | tf_op jit(solution)/shard_map/all_to_all | solution.py:77
  77.3 149.0 %reduce-scatter.2.cloned.1.call-start = ((), (), s32[]{:S(2)}) async-start(), calls=%async_computation.5 | async-start | bytes 3276800 | tf_op jit(solution)/shard_map/reduce_scatter | solution.py:109
  124.2 2.1 copy-start.3
  126.3 13.1 %copy-start.1 = (f32[2,20,64,128]{3,2,1,0:T(8,128)S(1)}, f32[2,20,64,128]{3,2,1,0:T(8,128)}, u32[]{:S(2)}) copy-start(f32[2,20,64,128]{3,2,1,0:T(8,128)} %get-tuple-element.127) | copy-start | bytes 3932164
  157.9 8.9 %copy-start.4 = (f32[3,8,2,256]{3,1,2,0:T(8,128)S(1)}, f32[3,8,2,256]{3,1,2,0:T(8,128)}, u32[]{:S(2)}) copy-start(f32[3,8,2,256]{3,1,2,0:T(8,128)} %copy.75) | copy-start | bytes 147460
  157.9 8.9 %copy-start.7 = (f32[20]{0:T(128)S(1)}, f32[20]{0:T(128)}, u32[]{:S(2)}) copy-start(f32[20]{0:T(128)} %param.19) | copy-start | bytes 244
  173.7 9.2 %copy-start.6 = (f32[1280]{0:T(1024)S(1)}, f32[1280]{0:T(1024)}, u32[]{:S(2)}) copy-start(f32[1280]{0:T(1024)} %param.20) | copy-start | bytes 15364
Sparse Core Ops, SparseCore 0:
  70.6 87.2 all-gather.3
  193.3 32.9 reduce-scatter.1
where the time goes:
time: 235 us; the launch traced here: 233 us
  waiting for transfers between devices  54.3 us (23%)
  blocking collectives  51.9 us (22%)
  local copies, waits for them, and re-layouts  38.9 us (17%)
  matrix products  32.5 us (14%)
  other arithmetic  25.6 us (11%)
  starting transfers between devices  15.4 us (7%)
  between operations  14.3 us (6%)
    reduce_scatter x1, waiting for transfers between devices, local(): lax.psum_scatter(jnp.dot(normed, out_weight, preferred_element_type=jnp.f...  33.1 us
    unnamed x1, blocking collectives  22.7 us
    all_gather x1, blocking collectives, local(): lax.all_gather(c_proj, 'grp', axis=0, tiled=True)  17.5 us
    all_to_all x1, waiting for transfers between devices, local(): lax.all_to_all(channels, 'grp', split_axis=1, concat_axis=0, tiled=True)  15.3 us
    dot_general x1, matrix products, local_scan(): y_intra = jnp.einsum('qhij,qjhp->qihp', weights, inputs, precision=highest)  13.1 us
    convert_element_type x3, local copies, waits for them, and re-layouts, local_scan(): chan_f = chan_heads.astype(jnp.float32).reshape(piece_len, nheads, HD)  10.9 us
    select_n x7, other arithmetic, turn(): jnp.where(position < mine, new, old)  8.64 us
    convert_element_type x2, local copies, waits for them, and re-layouts, local(): gate_heads.astype(jnp.float32)  8.27 us
  transfers between devices with their start and end apart: 6, of which 4 were waited for; matrix products, arithmetic and copies ran while one was open for 19% of the time, Pallas kernels for 0%

commit v1 on v0

--- a/solution.py
+++ b/solution.py
@@ -75,7 +75,12 @@
     chan_heads, gate_heads, step_heads, decay_heads = (
         lax.all_to_all(channels, "grp", split_axis=1, concat_axis=0, tiled=True),
         lax.all_to_all(gates, "grp", split_axis=1, concat_axis=0, tiled=True),
-        lax.all_to_all(step_size, "grp", split_axis=1, concat_axis=0, tiled=True),
+        jnp.concatenate(
+            lax.all_to_all(
+                jnp.stack(jnp.split(step_size, lax.axis_size("grp"), axis=1)), "grp", 0, 0
+            ),
+            axis=0,
+        ),
         lax.all_to_all(log_decay, "grp", split_axis=1, concat_axis=0, tiled=True),
     )
     b_rows, c_rows = (

time: 235 us -> 235 us (level)
    unnamed x25 -> x23, local copies, waits for them, and re-layouts: 7.84 us -> 7.84 us
  transfers between devices with their start and end apart: 6 -> 6, of which waited for: 4 -> 4; matrix products, arithmetic and copies ran while one was open for 19% -> 20% of each run, Pallas kernels for 0% -> 0%
where the time goes in v1:
time: 235 us; the launch traced here: 234 us
  waiting for transfers between devices  54.3 us (23%)
  blocking collectives  51.9 us (22%)
  local copies, waits for them, and re-layouts  39 us (17%)
  matrix products  32.4 us (14%)
  other arithmetic  26.2 us (11%)
  starting transfers between devices  15.4 us (7%)
  between operations  14.3 us (6%)
    reduce_scatter x1, waiting for transfers between devices, local(): lax.psum_scatter(jnp.dot(normed, out_weight, preferred_element_type=jnp.f...  33.1 us
    unnamed x1, blocking collectives  22.7 us
    all_gather x1, blocking collectives, local(): lax.all_gather(c_proj, 'grp', axis=0, tiled=True)  17.5 us
    all_to_all x1, waiting for transfers between devices, local(): lax.all_to_all(channels, 'grp', split_axis=1, concat_axis=0, tiled=True)  15.1 us
    dot_general x1, matrix products, local_scan(): y_intra = jnp.einsum('qhij,qjhp->qihp', weights, inputs, precision=highest)  13.1 us
    convert_element_type x3, local copies, waits for them, and re-layouts, local_scan(): chan_f = chan_heads.astype(jnp.float32).reshape(piece_len, nheads, HD)  10.9 us
    select_n x7, other arithmetic, turn(): jnp.where(position < mine, new, old)  8.64 us
    convert_element_type x2, local copies, waits for them, and re-layouts, local(): gate_heads.astype(jnp.float32)  8.27 us
  transfers between devices with their start and end apart: 6, of which 4 were waited for; matrix products, arithmetic and copies ran while one was open for 20% of the time, Pallas kernels for 0%

profile of v1, /device:TPU:0, one launch (start us, length us, event | category | flops | bytes accessed | tf_op | source)
XLA Modules:
  0.0 233.9 jit_solution(3611515277049778883)
XLA Ops:
  7.9 4.2 %all-to-all-start.2 = ((bf16[128,4,20]{0,2,1:T(8,128)(2,1)}), bf16[128,4,20]{0,2,1:T(8,128)(2,1)S(1)}, u32[]{:S(2)}, u32[]{:S(2)}) async-start(bf16[128,4,20]{0,2,1:T(8,128)(2,1)} %all_to_all.36), calls=%async_computation.2 | async-start | bytes 49152 | tf_op jit(solution)/shard_map/all_to_all | solution.py:84
  13.5 5.8 %all_gather.17 = bf16[512,128]{1,0:T(8,128)(2,1)S(1)} all-gather(bf16[128,128]{1,0:T(8,128)(2,1)} %param.15), channel_id=1, replica_groups=mesh['ctx'=8,'grp'=4] {'grp'}, dimensions={0}, use_global_device_ids=true | all-gather | bytes 163840 | tf_op jit(solution)/shard_map/all_gather | solution.py:87
  21.7 3.3 %all-to-all-start.1 = ((bf16[4,128,20]{1,2,0:T(8,128)(2,1)}), bf16[4,128,20]{1,2,0:T(8,128)(2,1)S(1)}, u32[]{:S(2)}, u32[]{:S(2)}) async-start(bf16[4,128,20]{1,2,0:T(8,128)(2,1)} %pad_maximum_fusion), calls=%async_computation.1 | async-start | bytes 49152 | tf_op jit(solution)/shard_map/all_to_all | solution.py:79
  26.3 2.5 %all-to-all-done.1 = bf16[4,128,20]{1,2,0:T(8,128)(2,1)S(1)} async-done(((bf16[4,128,20]{1,2,0:T(8,128)(2,1)}), bf16[4,128,20]{1,2,0:T(8,128)(2,1)S(1)}, u32[]{:S(2)}, u32[]{:S(2)}) %all-to-all-start.1) | async-done | bytes 20512 | tf_op jit(solution)/shard_map/all_to_all | solution.py:79
  28.8 3.5 %all-to-all-start = ((bf16[128,4,1280]{0,2,1:T(8,128)(2,1)}), bf16[128,4,1280]{0,2,1:T(8,128)(2,1)S(1)}, u32[]{:S(2)}, u32[]{:S(2)}) async-start(bf16[128,4,1280]{0,2,1:T(8,128)(2,1)} %bitcast), calls=%async_computation | async-start | bytes 2621440 | tf_op jit(solution)/shard_map/all_to_all | solution.py:76
  34.5 15.1 %all-to-all-done = bf16[128,4,1280]{0,2,1:T(8,128)(2,1)S(1)} async-done(((bf16[128,4,1280]{0,2,1:T(8,128)(2,1)}), bf16[128,4,1280]{0,2,1:T(8,128)(2,1)S(1)}, u32[]{:S(2)}, u32[]{:S(2)}) %all-to-all-start) | async-done | bytes 1310752 | tf_op jit(solution)/shard_map/all_to_all | solution.py:76
  49.8 5.4 %copy.52 = f32[4,128,1280]{1,0,2:T(4,128)S(1)} copy(f32[4,128,1280]{1,2,0:T(8,128)S(1)} %convert_bitcast_fusion.1) | data formatting | bytes 5242880 | tf_op jit(solution)/shard_map/convert_element_type | solution.py:33
  55.2 3.3 %reshape.120 = f32[2,256,20,64]{1,0,3,2:T(2,128)} reshape(f32[4,128,1280]{1,0,2:T(4,128)S(1)} %copy.52) | data formatting | bytes 5242880 | tf_op jit(solution)/shard_map/convert_element_type | solution.py:33
  58.5 5.1 %broadcast_multiply_fusion = (f32[2,256,20,64]{1,0,3,2:T(2,128)S(1)}, f32[2,256,20,64]{1,0,3,2:T(2,128)}) fusion(f32[2,256,20]{1,0,2:T(2,128)S(1)} %get-tuple-element.189, f32[2,256,20,64]{1,0,3,2:T(2,128)} %reshape.120, f32[2,256,20]{1,0,2:T(2,128)S(1)} %reshape.121), kind=kLoop, calls=%fused_computation.39 | loop fusion | flops 1310720 | bytes 7946240 | tf_op jit(solution)/shard_map/mul | solution.py:50
  66.0 4.3 %while.27 = (s32[]{:T(128)}, f32[20,64,128]{2,1,0:T(8,128)S(1)}, f32[2,20,64,128]{3,2,1,0:T(8,128)}, f32[2,20]{1,0:T(2,128)S(1)}, f32[2,20,64,128]{3,2,1,0:T(8,128)}, /*index=5*/s32[]{:T(128)}, s32[]{:T(128)}) while((s32[]{:T(128)}, f32[20,64,128]{2,1,0:T(8,128)S(1)}, f32[2,20,64,128]{3,2,1,0:T(8,128)}, f32[2,20]{1,0:T(2,128)S(1)}, ...), condition=%wide.region_3.4_spmd.clone, body=%wide.region_2.3_spmd.clone.sunk | while | flops 655363 | bytes 3277648 | solution.py:58
  73.7 4.3 %all-to-all-start.3 = ((bf16[128,4,1280]{0,2,1:T(8,128)(2,1)}), bf16[128,4,1280]{0,2,1:T(8,128)(2,1)}, u32[]{:S(2)}, u32[]{:S(2)}) async-start(bf16[128,4,1280]{0,2,1:T(8,128)(2,1)} %bitcast.131), calls=%async_computation.3 | async-start | bytes 2621440 | tf_op jit(solution)/shard_map/all_to_all | solution.py:77
  79.3 17.5 %all_gather.16 = bf16[512,128]{1,0:T(8,128)(2,1)S(1)} all-gather(bf16[128,128]{1,0:T(8,128)(2,1)} %param.16), channel_id=1, replica_groups=mesh['ctx'=8,'grp'=4] {'grp'}, dimensions={0}, use_global_device_ids=true | all-gather | bytes 163840 | tf_op jit(solution)/shard_map/all_gather | solution.py:88
  100.7 22.7 %all-reduce = f32[160]{0:T(256)S(1)} all-reduce(f32[160]{0:T(256)S(1)} %exponential_dynamic-update-slice_fusion), channel_id=2, replica_groups=mesh['ctx'=8,'grp'=4] {'ctx'}, use_global_device_ids=true, to_apply=%add | all-reduce | flops 160 | bytes 1280
  127.1 13.1 %fusion.2 = f32[2,20,64,256]{3,2,1,0:T(8,128)S(1)} fusion(f32[2,256,256]{2,1,0:T(8,128)} %fusion.28, f32[2,20,256]{2,1,0:T(8,128)} %copy.57, pred[256,256]{1,0:T(8,128)(4,1)S(1)} %copy-done.3, f32[2,256,20,64]{1,0,3,2:T(2,128)} %get-tuple-element.187), kind=kOutput, calls=%fused_computation.7 | convolution fusion | flops 2021130240 | bytes 5873664 | tf_op jit(solution)/shard_map/qhij,qjhp->qihp/dot_general | solution.py:45
  146.8 4.1 %copy.71 = f32[4,128,1280]{1,0,2:T(4,128)} copy(f32[4,128,1280]{2,1,0:T(8,128)} %convert_bitcast_fusion) | data formatting | bytes 5242880 | tf_op jit(solution)/shard_map/convert_element_type | solution.py:109
  151.0 4.1 %reshape.125 = f32[512,20,64]{0,2,1:T(8,128)} reshape(f32[4,128,1280]{1,0,2:T(4,128)} %copy.71) | data formatting | bytes 5242880 | tf_op jit(solution)/shard_map/convert_element_type | solution.py:109
  155.1 3.5 %all-gather.4.cloned.1.call-done = f32[160,64,128]{2,1,0:T(8,128)} async-done(((f32[20,64,128]{2,1,0:T(8,128)}), f32[160,64,128]{2,1,0:T(8,128)}) %all-gather.4.cloned.1.call-update) | async-done | bytes 5242896 | tf_op jit(solution)/shard_map/all_gather | solution.py:14
  158.6 8.9 %while.28 = (s32[]{:T(128)}, f32[20,64,128]{2,1,0:T(8,128)S(1)}, s32[]{:T(128)}, f32[8,20]{1,0:T(8,128)S(1)}, f32[8,20,64,128]{3,2,1,0:T(8,128)}, /*index=5*/s32[]{:T(128)}, s32[]{:T(128)}) while((s32[]{:T(128)}, f32[20,64,128]{2,1,0:T(8,128)S(1)}, s32[]{:T(128)}, f32[8,20]{1,0:T(8,128)S(1)}, f32[8,20,64,128]{3,2,1,0:T(8,128)}, ...), condition=%wide.region_6.7_spmd.clone, body=%wide.region_5.6_spmd.clone.sunk | while | flops 655364 | bytes 1966425 | solution.py:23
  167.6 6.9 %multiply_reduce_fusion = (f32[512]{0:T(512)S(1)}, f32[512,20,64]{0,2,1:T(8,128)}) fusion(f32[512,20,64]{0,2,1:T(8,128)} %reshape.125, f32[512,20,64]{0,2,1:T(8,128)} %reshape.123, f32[20]{0:T(128)S(1)} %copy-done.6, f32[512,20,64]{0,2,1:T(8,128)} %bitcast.132, f32[512,20]{0,1:T(8,128)S(1)} %bitcast.143, f32[20,64,128]{2,1,0:T(8,128)S(1)} %get-tuple-element.129, ...), kind=kOutput, calls=%fused_computation.37 | convolution fusion | flops 1013841408 | bytes 11315280 | tf_op jit(solution)/shard_map/tn,hpn->thp/dot_general | solution.py:104
  174.4 3.2 %copy.70 = f32[512,1280]{1,0:T(8,128)} copy(f32[512,1280]{0,1:T(8,128)} %bitcast.133) | data formatting | bytes 5242880 | tf_op jit(solution)/shard_map/reshape | solution.py:108
  177.7 5.9 %psum.7 = f32[512]{0:T(512)S(1)} all-reduce(f32[512]{0:T(512)S(1)} %get-tuple-element.197), channel_id=1, replica_groups=mesh['ctx'=8,'grp'=4] {'grp'}, use_global_device_ids=true, to_apply=%region_9.10 | all-reduce | flops 512 | bytes 4096 | tf_op jit(solution)/shard_map/psum | solution.py:111
  183.6 2.6 %fusion.25 = bf16[512,1280]{1,0:T(8,128)(2,1)S(1)} fusion(f32[512,1280]{1,0:T(8,128)} %copy.70, bf16[128,4,1280]{2,0,1:T(8,128)(2,1)S(1)} %copy.69, f32[1280]{0:T(1024)S(1)} %copy-done.5, f32[512]{0:T(512)S(1)} %add_rsqrt_fusion), kind=kLoop, calls=%fused_computation.38 | loop fusion | flops 5898240 | bytes 5250048 | tf_op jit(solution)/shard_map/convert_element_type | solution.py:113
  186.2 7.7 %convolution_convert_fusion = bf16[512,2560]{1,0:T(8,128)(2,1)} fusion(bf16[512,1280]{1,0:T(8,128)(2,1)S(1)} %fusion.25, bf16[1280,2560]{1,0:T(8,128)(2,1)} %param.21), kind=kOutput, calls=%fused_computation.17 | convolution fusion | flops 3356753920 | bytes 10485760 | tf_op jit(solution)/shard_map/dot_general | solution.py:115
  193.9 33.1 %reduce-scatter.2.cloned.1.call-done = bf16[128,2560]{1,0:T(8,128)(2,1)} async-done(((bf16[512,2560]{1,0:T(8,128)(2,1)}), bf16[128,2560]{1,0:T(8,128)(2,1)}) %reduce-scatter.2.cloned.1.call-update) | async-done | bytes 655376 | tf_op jit(solution)/shard_map/reduce_scatter | solution.py:114
  (91 shorter events, 42.1 us)
Async XLA Ops:
  7.9 13.8 %all-to-all-start.2 = ((bf16[128,4,20]{0,2,1:T(8,128)(2,1)}), bf16[128,4,20]{0,2,1:T(8,128)(2,1)S(1)}, u32[]{:S(2)}, u32[]{:S(2)}) async-start(bf16[128,4,20]{0,2,1:T(8,128)(2,1)} %all_to_all.36), calls=%async_computation.2 | async-start | bytes 49152 | tf_op jit(solution)/shard_map/all_to_all | solution.py:84
  21.7 7.1 %all-to-all-start.1 = ((bf16[4,128,20]{1,2,0:T(8,128)(2,1)}), bf16[4,128,20]{1,2,0:T(8,128)(2,1)S(1)}, u32[]{:S(2)}, u32[]{:S(2)}) async-start(bf16[4,128,20]{1,2,0:T(8,128)(2,1)} %pad_maximum_fusion), calls=%async_computation.1 | async-start | bytes 49152 | tf_op jit(solution)/shard_map/all_to_all | solution.py:79
  28.8 20.8 %all-to-all-start = ((bf16[128,4,1280]{0,2,1:T(8,128)(2,1)}), bf16[128,4,1280]{0,2,1:T(8,128)(2,1)S(1)}, u32[]{:S(2)}, u32[]{:S(2)}) async-start(bf16[128,4,1280]{0,2,1:T(8,128)(2,1)} %bitcast), calls=%async_computation | async-start | bytes 2621440 | tf_op jit(solution)/shard_map/all_to_all | solution.py:76
  32.4 126.3 %all-gather.4.cloned.1.call-start = ((), (), s32[]{:S(2)}) async-start(), calls=%async_computation.6 | async-start | bytes 5898240 | tf_op jit(solution)/shard_map/all_gather | solution.py:14
  32.8 16.8 %copy-start.2 = (f32[2,20,256]{2,0,1:T(2,128)}, f32[2,20,256]{2,0,1:T(2,128)S(1)}, u32[]{:S(2)}) copy-start(f32[2,20,256]{2,0,1:T(2,128)S(1)} %reduce_window_sum.35) | copy-start | bytes 122884
  70.4 0.8 copy-start
  71.2 6.9 %copy-start.7 = (u32[32]{0:T(128)S(1)}, u32[32]{0:T(128)}, u32[]{:S(2)}) copy-start(u32[32]{0:T(128)} %constant.61) | copy-start | bytes 388
  73.7 69.8 %all-to-all-start.3 = ((bf16[128,4,1280]{0,2,1:T(8,128)(2,1)}), bf16[128,4,1280]{0,2,1:T(8,128)(2,1)}, u32[]{:S(2)}, u32[]{:S(2)}) async-start(bf16[128,4,1280]{0,2,1:T(8,128)(2,1)} %bitcast.131), calls=%async_computation.3 | async-start | bytes 2621440 | tf_op jit(solution)/shard_map/all_to_all | solution.py:77
  78.0 149.0 %reduce-scatter.2.cloned.1.call-start = ((), (), s32[]{:S(2)}) async-start(), calls=%async_computation.5 | async-start | bytes 3276800 | tf_op jit(solution)/shard_map/reduce_scatter | solution.py:114
  125.0 2.1 copy-start.3
  127.1 13.1 %copy-start.1 = (f32[2,20,64,128]{3,2,1,0:T(8,128)S(1)}, f32[2,20,64,128]{3,2,1,0:T(8,128)}, u32[]{:S(2)}) copy-start(f32[2,20,64,128]{3,2,1,0:T(8,128)} %get-tuple-element.127) | copy-start | bytes 3932164
  158.6 8.9 %copy-start.4 = (f32[3,8,2,256]{3,1,2,0:T(8,128)S(1)}, f32[3,8,2,256]{3,1,2,0:T(8,128)}, u32[]{:S(2)}) copy-start(f32[3,8,2,256]{3,1,2,0:T(8,128)} %copy.75) | copy-start | bytes 147460
  158.6 8.9 %copy-start.6 = (f32[20]{0:T(128)S(1)}, f32[20]{0:T(128)}, u32[]{:S(2)}) copy-start(f32[20]{0:T(128)} %param.19) | copy-start | bytes 244
  174.4 9.2 %copy-start.5 = (f32[1280]{0:T(1024)S(1)}, f32[1280]{0:T(1024)}, u32[]{:S(2)}) copy-start(f32[1280]{0:T(1024)} %param.20) | copy-start | bytes 15364
Sparse Core Ops, SparseCore 0:
  71.3 87.2 all-gather.3
  194.1 32.9 reduce-scatter.1
